TPU v7x, 128 devices: a whole 4x4x4 slice. The times are simulated.
128 devices in a mesh: clip: 16 (over y, x), feat: 8 (over z, core).
Axes of the slice: x: 4, y: 4, z: 4, core: 2. Of those that a mesh axis runs over, the one named last changes fastest.
Arguments:
- features: float32 [12288, 22528], P('clip', 'feat'), may hold values from -20 to 20
- weights: float32 [400, 22528], P(None, 'feat'), may hold values from -0.02665009 to 0.02665009
- labels: int32 [12288], P('clip'), may hold values from 0 to 399
Outputs:
- new_weights: float32 [400, 22528], P(None, 'feat')
- residual: float32 [400, 22528], P(None, 'feat')
All inputs are finite; a program needn't handle non-finite values.
Results may differ from a plain program's by a relative error of at most 0.0003.
Values sent between devices are 32-bit elements; how exact they have to be, the bound alone decides.
A program may use at most 128 MiB of HBM per device.

v0:
```python
import jax
import jax.numpy as jnp
from jax import lax
from jax.sharding import PartitionSpec as P

ITERS = 2


damping = 0.01


def cut_along(array, dim, count):
    dims = array.shape
    blocks = array.reshape(*dims[:dim], count, dims[dim] // count, *dims[dim + 1 :])
    return jnp.moveaxis(blocks, dim, 0)


def sent_and_summed(array, axis, dim):
    blocks = cut_along(array, dim, lax.axis_size(axis))
    arrived = lax.all_to_all(blocks, axis, split_axis=0, concat_axis=0, tiled=True)
    return arrived.sum(axis=0)


def in_order(blocks, dim):
    blocks = jnp.moveaxis(blocks, 0, dim)
    dims = blocks.shape
    return blocks.reshape(*dims[:dim], dims[dim] * dims[dim + 1], *dims[dim + 2 :])


def from_everyone(array, axis):
    count = lax.axis_size(axis)
    return lax.all_to_all(
        jnp.broadcast_to(array[None], (count, *array.shape)), axis, 0, 0, tiled=True
    )


def gathered_copies(array, axis, dim):
    return in_order(from_everyone(array, axis), dim)


def contract_rows(left, right):
    return lax.dot_general(
        left,
        right,
        (((0,), (0,)), ((), ())),
        precision=lax.Precision.HIGHEST,
        preferred_element_type=jnp.float32,
    )


def contract_feats(left, right):
    return lax.dot_general(
        left,
        right,
        (((1,), (1,)), ((), ())),
        precision=lax.Precision.HIGHEST,
        preferred_element_type=jnp.float32,
    )


def local(features, weights, labels):
    rows_dev = features.shape[0]
    classes = weights.shape[0]
    total_rows = rows_dev * lax.axis_size("clip")
    row_share = rows_dev // lax.axis_size("feat")
    my_labels = lax.dynamic_slice_in_dim(labels, lax.axis_index("feat") * row_share, row_share)

    def reduce_rows(partial_sum):
        return sent_and_summed(partial_sum, "feat", 0)

    def spread_rows(row_values):
        return gathered_copies(row_values, "feat", 0)

    def backward(row_values):
        return lax.psum(contract_rows(row_values, features) / total_rows, "clip")

    logits = reduce_rows(contract_feats(features, weights))
    probs = jax.nn.softmax(logits, axis=1)
    onehot = (my_labels[:, None] == jnp.arange(classes, dtype=jnp.int32)[None, :]).astype(
        jnp.float32
    )
    gradient = backward(spread_rows(probs - onehot))
    residual = -gradient
    solution = jnp.zeros_like(residual)
    direction = residual
    for iteration in range(ITERS):
        tangent = reduce_rows(contract_feats(features, direction))
        bent = probs * tangent - probs * jnp.sum(probs * tangent, axis=1, keepdims=True)
        image = backward(spread_rows(bent)) + damping * direction
        norm_now, curvature, cross_term, image_norm = lax.psum(
            (
                jnp.sum(residual * residual),
                jnp.sum(direction * image),
                jnp.sum(residual * image),
                jnp.sum(image * image),
            ),
            "feat",
        )
        step_size = norm_now / curvature
        norm_next = norm_now - 2.0 * step_size * cross_term + step_size * step_size * image_norm
        solution = solution + step_size * direction
        residual = residual - step_size * image
        direction = residual + norm_next / norm_now * direction
    return (weights + solution, residual)


def solution(mesh):
    in_specs = (P("clip", "feat"), P(None, "feat"), P("clip"))
    out_specs = (P(None, "feat"), P(None, "feat"))
    return jax.shard_map(local, mesh=mesh, in_specs=in_specs, out_specs=out_specs, check_vma=False)
```

profile of v0, /device:TPU:0, one launch (start us, length us, event | category | flops | bytes accessed | tf_op | source)
XLA Modules:
  0.0 636.5 jit_solution(7377820239955165576)
XLA Ops:
  7.2 18.5 %fusion.11 = f32[768,400]{1,0:T(8,128)} fusion(f32[768,2816]{1,0:T(8,128)} %param.3, f32[400,2816]{1,0:T(8,128)} %param.4), kind=kOutput, calls=%fused_computation.29 | convolution fusion | flops 10380902400 | bytes 14385152 | tf_op jit(solution)/shard_map/reshape | solution.py:14
  25.7 5.4 all-to-all-start
  31.1 0.0 all-reduce.6.cloned.1.call-start
  31.2 0.8 dynamic_slice.3
  31.9 20.7 %all-to-all-done = f32[8,96,400]{2,1,0:T(8,128)S(1)} async-done(((f32[8,96,400]{2,1,0:T(8,128)}), f32[8,96,400]{2,1,0:T(8,128)S(1)}, u32[]{:S(2)}, u32[]{:S(2)}) %all-to-all-start) | async-done | bytes 1228832 | tf_op jit(solution)/shard_map/all_to_all | solution.py:20
  52.7 0.1 reduce_sum.103
  52.8 0.1 copy.17
  52.9 0.1 reduce_max.9
  53.1 0.1 fusion.6
  53.1 0.1 convert_subtract_fusion
  53.2 0.1 copy.7
  53.3 0.2 broadcast_in_dim.6
  53.5 24.0 %all_to_all.30 = f32[8,96,400]{2,1,0:T(8,128)S(1)} all-to-all(f32[8,96,400]{2,1,0:T(8,128)S(1)} %broadcast_in_dim.6), channel_id=1, replica_groups=mesh['clip'=16,'feat'=8] {'feat'}, dimensions={0} | all-to-all | bytes 2457600 | tf_op jit(solution)/shard_map/all_to_all | solution.py:32
  77.6 16.0 %convolution_multiply_fusion.2 = f32[400,2816]{1,0:T(8,128)} fusion(f32[768,400]{1,0:T(8,128)S(1)} %bitcast.22, f32[768,2816]{1,0:T(8,128)} %param.3), kind=kOutput, calls=%fused_computation.2 | convolution fusion | flops 10382028800 | bytes 14385152 | tf_op jit(solution)/shard_map/dot_general | solution.py:42
  93.6 0.0 all-reduce.6.cloned.1.call-update
  93.6 0.2 all-reduce.8.cloned.1.call-start
  93.8 105.4 %all-reduce.6.cloned.1.call-done = f32[400,2816]{1,0:T(8,128)} async-done(((f32[400,2816]{1,0:T(8,128)}), f32[400,2816]{1,0:T(8,128)}) %all-reduce.6.cloned.1.call-update) | async-done | bytes 4505616 | tf_op jit(solution)/shard_map/psum | solution.py:75
  199.3 14.9 %fusion.2 = f32[768,400]{0,1:T(8,128)S(1)} fusion(f32[768,2816]{1,0:T(8,128)} %param.3, f32[400,2816]{1,0:T(8,128)} %all-reduce.6.cloned.1.call-done), kind=kOutput, calls=%fused_computation.16 | convolution fusion | flops 10382028800 | bytes 14385152 | tf_op jit(solution)/shard_map/dot_general | solution.py:52
  214.2 0.5 copy.15
  214.7 25.8 %all_to_all.31 = f32[8,96,400]{2,1,0:T(8,128)S(1)} all-to-all(f32[8,96,400]{2,1,0:T(8,128)S(1)} %bitcast.20), channel_id=1, replica_groups=mesh['clip'=16,'feat'=8] {'feat'}, dimensions={0} | all-to-all | bytes 2457600 | tf_op jit(solution)/shard_map/all_to_all | solution.py:20
  240.5 0.1 reduce_sum.106
  240.6 0.1 copy.19
  240.8 0.1 fusion.9
  240.8 0.1 multiply_subtract_fusion.3
  240.9 0.1 copy.10
  241.0 0.2 broadcast_in_dim.7
  241.2 24.0 %all_to_all.32 = f32[8,96,400]{2,1,0:T(8,128)S(1)} all-to-all(f32[8,96,400]{2,1,0:T(8,128)S(1)} %broadcast_in_dim.7), channel_id=1, replica_groups=mesh['clip'=16,'feat'=8] {'feat'}, dimensions={0} | all-to-all | bytes 2457600 | tf_op jit(solution)/shard_map/all_to_all | solution.py:32
  265.3 16.0 %convolution_multiply_fusion.1 = f32[400,2816]{1,0:T(8,128)} fusion(f32[768,400]{1,0:T(8,128)S(1)} %bitcast.23, f32[768,2816]{1,0:T(8,128)} %param.3), kind=kOutput, calls=%fused_computation.1 | convolution fusion | flops 10382028800 | bytes 14385152 | tf_op jit(solution)/shard_map/dot_general | solution.py:42
  281.3 0.0 all-reduce.8.cloned.1.call-update
  281.3 0.3 all-reduce.10.cloned.1.call-start
  281.6 103.7 %all-reduce.8.cloned.1.call-done = f32[400,2816]{1,0:T(8,128)} async-done(((f32[400,2816]{1,0:T(8,128)}), f32[400,2816]{1,0:T(8,128)}) %all-reduce.8.cloned.1.call-update) | async-done | bytes 4505616 | tf_op jit(solution)/shard_map/psum | solution.py:75
  385.2 5.6 multiply_reduce_fusion.1
  390.8 15.3 %all-reduce.1 = (f32[]{:T(128)}, f32[]{:T(128)}, f32[]{:T(128)}) all-reduce(f32[]{:T(128)} %get-tuple-element.6, f32[]{:T(128)} %get-tuple-element.5, f32[]{:T(128)} %get-tuple-element.4), channel_id=1, replica_groups=mesh['clip'=16,'feat'=8] {'feat'}, use_global_device_ids=true, to_apply=%region_5.0 | all-reduce | flops 3 | bytes 24 | tf_op jit(solution)/shard_map/psum | solution.py:90
  410.0 16.4 %convolution_bitcast_fusion = f32[768,400]{0,1:T(8,128)S(1)} fusion(f32[768,2816]{1,0:T(8,128)} %param.3, f32[400,2816]{1,0:T(8,128)} %all-reduce.6.cloned.1.call-done, f32[]{:T(128)S(6)} %div.41, f32[400,2816]{1,0:T(8,128)} %all-reduce.8.cloned.1.call-done, f32[]{:T(128)S(6)} %div.40), kind=kOutput, calls=%fused_computation.17 | convolution fusion | flops 10388787200 | bytes 18890760 | tf_op jit(solution)/shard_map/dot_general | solution.py:52
  426.4 0.5 copy.16
  426.9 24.0 %all_to_all.33 = f32[8,96,400]{2,1,0:T(8,128)S(1)} all-to-all(f32[8,96,400]{2,1,0:T(8,128)S(1)} %bitcast.21), channel_id=1, replica_groups=mesh['clip'=16,'feat'=8] {'feat'}, dimensions={0} | all-to-all | bytes 2457600 | tf_op jit(solution)/shard_map/all_to_all | solution.py:20
  450.9 0.1 reduce_sum.111
  451.1 0.1 copy.20
  451.2 0.1 fusion.10
  451.3 0.1 multiply_subtract_fusion.2
  451.3 0.1 copy.13
  451.5 0.2 broadcast_in_dim.8
  451.7 24.3 %all_to_all.34 = f32[8,96,400]{2,1,0:T(8,128)S(1)} all-to-all(f32[8,96,400]{2,1,0:T(8,128)S(1)} %broadcast_in_dim.8), channel_id=1, replica_groups=mesh['clip'=16,'feat'=8] {'feat'}, dimensions={0} | all-to-all | bytes 2457600 | tf_op jit(solution)/shard_map/all_to_all | solution.py:32
  475.9 16.0 %convolution_multiply_fusion = f32[400,2816]{1,0:T(8,128)} fusion(f32[768,400]{1,0:T(8,128)S(1)} %bitcast.24, f32[768,2816]{1,0:T(8,128)} %param.3), kind=kOutput, calls=%fused_computation | convolution fusion | flops 10382028800 | bytes 14385152 | tf_op jit(solution)/shard_map/dot_general | solution.py:42
  491.9 0.0 all-reduce.10.cloned.1.call-update
  492.0 104.0 %all-reduce.10.cloned.1.call-done = f32[400,2816]{1,0:T(8,128)} async-done(((f32[400,2816]{1,0:T(8,128)}), f32[400,2816]{1,0:T(8,128)}) %all-reduce.10.cloned.1.call-update) | async-done | bytes 4505616 | tf_op jit(solution)/shard_map/psum | solution.py:75
  595.9 6.5 %multiply_reduce_fusion = (f32[]{:T(128)}, f32[]{:T(128)}) fusion(f32[400,2816]{1,0:T(8,128)} %all-reduce.10.cloned.1.call-done, f32[400,2816]{1,0:T(8,128)} %all-reduce.6.cloned.1.call-done, f32[]{:T(128)S(6)} %div.41, f32[400,2816]{1,0:T(8,128)} %all-reduce.8.cloned.1.call-done, f32[]{:T(128)S(6)} %div.40), kind=kLoop, calls=%fused_computation.5 | loop fusion | flops 14643198 | bytes 13516816 | tf_op jit(solution)/shard_map/reduce_sum | solution.py:93
  602.4 15.2 %all-reduce = (f32[]{:T(128)}, f32[]{:T(128)}) all-reduce(f32[]{:T(128)} %get-tuple-element.3, f32[]{:T(128)} %get-tuple-element.2), channel_id=1, replica_groups=mesh['clip'=16,'feat'=8] {'feat'}, use_global_device_ids=true, to_apply=%region_12.0 | all-reduce | flops 2 | bytes 16 | tf_op jit(solution)/shard_map/psum | solution.py:90
  619.0 10.6 %multiply_subtract_fusion = (f32[400,2816]{1,0:T(8,128)}, f32[400,2816]{1,0:T(8,128)}) fusion(f32[400,2816]{1,0:T(8,128)} %all-reduce.10.cloned.1.call-done, f32[]{:T(128)S(6)} %div.43, f32[400,2816]{1,0:T(8,128)} %all-reduce.6.cloned.1.call-done, f32[]{:T(128)S(6)} %div.41, f32[400,2816]{1,0:T(8,128)} %all-reduce.8.cloned.1.call-done, f32[]{:T(128)S(6)} %div.40, ...), kind=kLoop, calls=%fused_computation.3 | loop fusion | flops 16896000 | bytes 27033612 | tf_op jit(solution)/shard_map/sub | solution.py:102
Async XLA Ops:
  25.7 27.0 %all-to-all-start = ((f32[8,96,400]{2,1,0:T(8,128)}), f32[8,96,400]{2,1,0:T(8,128)S(1)}, u32[]{:S(2)}, u32[]{:S(2)}) async-start(f32[8,96,400]{2,1,0:T(8,128)} %bitcast), calls=%async_computation | async-start | bytes 3145728 | tf_op jit(solution)/shard_map/all_to_all | solution.py:20
  31.1 168.1 %all-reduce.6.cloned.1.call-start = ((), (), s32[]{:S(2)}) async-start(), calls=%async_computation.6 | async-start | bytes 9011200 | tf_op jit(solution)/shard_map/psum | solution.py:75
  93.6 291.6 %all-reduce.8.cloned.1.call-start = ((), (), s32[]{:S(2)}) async-start(), calls=%async_computation.7 | async-start | bytes 9011200 | tf_op jit(solution)/shard_map/psum | solution.py:75
  281.3 314.6 %all-reduce.10.cloned.1.call-start = ((), (), s32[]{:S(2)}) async-start(), calls=%async_computation.8 | async-start | bytes 9011200 | tf_op jit(solution)/shard_map/psum | solution.py:75
Sparse Core Ops, SparseCore 0:
  93.7 105.4 all-reduce.5
  281.4 103.7 all-reduce.7
  492.1 103.7 all-reduce.9
where the time goes:
time: 645 us; the launch traced here: 637 us
  waiting for transfers between devices  334 us (52%)
  blocking collectives  153 us (24%)
  matrix products  97.9 us (15%)
  other arithmetic  23.6 us (4%)
  between operations  19.6 us (3%)
    psum x3, waiting for transfers between devices, backward(): return lax.psum(contract_rows(row_values, features) / total_rows, 'clip')  313 us
    all_to_all x3, blocking collectives, from_everyone(): lax.all_to_all(jnp.broadcast_to(array[None], (count, *array.shape)), axis...  72.3 us
    all_to_all x2, blocking collectives, sent_and_summed(): lax.all_to_all(blocks, axis, split_axis=0, concat_axis=0, tiled=True)  49.8 us
    dot_general x3, matrix products, contract_rows(): lax.dot_general(left, right, (((0,), (0,)), ((), ())), precision=lax.Prec...  48 us
    dot_general x2, matrix products, contract_feats(): lax.dot_general(left, right, (((1,), (1,)), ((), ())), precision=lax.Prec...  31.3 us
    psum x2, blocking collectives, local(): lax.psum((jnp.sum(residual * residual), jnp.sum(direction * image), jnp.s...  30.5 us
    all_to_all x1, waiting for transfers between devices, sent_and_summed(): lax.all_to_all(blocks, axis, split_axis=0, concat_axis=0, tiled=True)  20.7 us
    reshape x1, matrix products, cut_along(): array.reshape(*dims[:dim], count, dims[dim] // count, *dims[dim + 1:])  18.5 us
  transfers between devices with their start and end apart: 4, of which 4 were waited for; matrix products, arithmetic and copies ran while one was open for 0% of the time, Pallas kernels for 0%

commit v1 on v0

v1 whole, which is shorter than its diff:
```python
import jax
import jax.numpy as jnp
from jax import lax
from jax.experimental import pallas as pl
from jax.experimental.pallas import tpu as pltpu
from jax.sharding import PartitionSpec as P

damping = 0.01

RING = 4
LANES = 128
ROW_BLOCKS = 3
TURNS = 3
STAGE = 128
SLOTS = 4
NT = (((1,), (1,)), ((), ()))
NN = (((1,), (0,)), ((), ()))


def up(value, unit):
    return -(-value // unit) * unit


def at(start, size):
    return pl.ds(start if isinstance(start, int) else pl.multiple_of(start, 8), size)


class Sems:
    def __init__(self, send, recv):
        self.send, self.recv, self.used = send, recv, 0

    def copy(self, src, dst, to):
        n = self.used
        self.used += 1
        return pltpu.make_async_remote_copy(
            src_ref=src,
            dst_ref=dst,
            send_sem=self.send.at[n],
            recv_sem=self.recv.at[n],
            device_id=to,
            device_id_type=pl.DeviceIdType.MESH,
        )


class Reduce:
    def __init__(self, sems, ring, work, start, seg, land, land_at):
        here, left, right = ring
        top = up(seg // 2, 8)
        low = seg - top
        self.work, self.start, self.seg, self.top, self.low = work, start, seg, top, low
        self.own, self.nxt, self.prv, opp = here, (here + 1) % 4, (here + 3) % 4, (here + 2) % 4
        self.relay_l = land.at[pl.ds(land_at, top)]
        self.relay_r = land.at[pl.ds(land_at + top, low)]
        l_top = land.at[pl.ds(land_at + seg, top)]
        l_low = land.at[pl.ds(land_at + seg + top, low)]
        r_top = land.at[pl.ds(land_at + 2 * seg, top)]
        r_low = land.at[pl.ds(land_at + 2 * seg + top, low)]
        self.landed = ((l_top, r_top), (l_low, r_low))

        def cp(s, off, size, dst, to):
            return sems.copy(work.at[self.rows(s, off, size)], dst, to)

        self.go_r = cp(opp, 0, top, self.relay_l, right)
        self.go_l = cp(opp, top, low, self.relay_r, left)
        self.near_r = cp(self.nxt, top, low, l_low, right)
        self.near_l = cp(self.prv, 0, top, r_top, left)
        self.sum_r = cp(self.nxt, 0, top, l_top, right)
        self.sum_l = cp(self.prv, top, low, r_low, left)

    def rows(self, s, off, size):
        return at(self.start + s * self.seg + off, size)

    def first(self):
        self.go_r.start()
        self.go_l.start()

    def near(self, wait):
        if wait:
            self.go_r.wait_send()
            self.go_l.wait_send()
        self.near_r.start()
        self.near_l.start()

    def second(self):
        self.go_r.wait_recv()
        rows = self.rows(self.nxt, 0, self.top)
        self.work[rows] = self.work[rows] + self.relay_l[...]
        self.sum_r.start()
        self.go_l.wait_recv()
        rows = self.rows(self.prv, self.top, self.low)
        self.work[rows] = self.work[rows] + self.relay_r[...]
        self.sum_l.start()

    def last(self, store):
        self.near_l.wait_recv()
        self.sum_r.wait_recv()
        a, b = self.landed[0]
        rows = self.rows(self.own, 0, self.top)
        store(rows, self.work[rows] + (a[...] + b[...]))
        self.near_r.wait_recv()
        self.sum_l.wait_recv()
        a, b = self.landed[1]
        rows = self.rows(self.own, self.top, self.low)
        store(rows, self.work[rows] + (a[...] + b[...]))

    def sent(self, waited):
        for c in (self.near_r, self.near_l, self.sum_r, self.sum_l) + (
            () if waited else (self.go_r, self.go_l)
        ):
            c.wait_send()


class Gather:
    def __init__(self, sems, ring, whole, start, seg):
        here, left, right = ring
        top = up(seg // 2, 8)
        low = seg - top
        nxt, prv = (here + 1) % 4, (here + 3) % 4

        def cp(s, off, size, to):
            ref = whole.at[at(start + s * seg + off, size)]
            return sems.copy(ref, ref, to)

        self.go_r = cp(here, 0, top, right)
        self.go_l = cp(here, top, low, left)
        self.near_r = cp(here, top, low, right)
        self.near_l = cp(here, 0, top, left)
        self.on_r = cp(prv, 0, top, right)
        self.on_l = cp(nxt, top, low, left)

    def first(self):
        self.go_r.start()
        self.go_l.start()

    def near(self, wait):
        if wait:
            self.go_r.wait_send()
            self.go_l.wait_send()
        self.near_r.start()
        self.near_l.start()

    def second(self):
        self.go_r.wait_recv()
        self.on_r.start()
        self.go_l.wait_recv()
        self.on_l.start()

    def last(self):
        self.near_r.wait_recv()
        self.near_l.wait_recv()
        self.on_r.wait_recv()
        self.on_l.wait_recv()

    def sent(self, waited):
        for c in (self.near_r, self.near_l, self.on_r, self.on_l) + (
            () if waited else (self.go_r, self.go_l)
        ):
            c.wait_send()


def tile_sum(value):
    return value.reshape(-1, 8, LANES).sum(axis=0)


def total(tile):
    return jnp.sum(jnp.sum(tile, axis=1, keepdims=True), axis=0, keepdims=True)


def split(value):
    high = value.astype(jnp.bfloat16)
    return high, (value - high.astype(jnp.float32)).astype(jnp.bfloat16)


def dot3(stack, size, right_hi, right_lo, dims):
    def dot(a, b):
        return lax.dot_general(a, b, dims, preferred_element_type=jnp.float32)

    both = dot(stack, right_hi)
    return both[:size] + (both[size:] + dot(stack[:size], right_lo))


class Sizes:
    def __init__(self, rows_dev, feats_dev, classes):
        first = up(classes // 2, 16)
        self.chunks = (first, classes - first)
        self.offs = (0, first)
        self.blocks = feats_dev // LANES
        self.row_lanes = rows_dev // LANES
        self.rb_rows = rows_dev // ROW_BLOCKS
        self.rb_blocks = self.rb_rows // LANES
        self.sub = [up(self.blocks * c + 8, 2 * 16 * 8) // 32 for c in self.chunks]
        self.seg = [s * RING for s in self.sub]
        self.side = [s * RING for s in self.seg]
        self.mark = [self.blocks * c for c in self.chunks]
        self.zmark = [self.rb_blocks * c for c in self.chunks]
        self.zseg = [up(m + 16, 2 * RING * 8) // (2 * RING) for m in self.zmark]
        self.zhalf = [s * RING for s in self.zseg]
        self.zall = [s * 2 for s in self.zhalf]


def make_kernel(s, rows_dev, classes, total_rows):
    def kernel(f_hbm, w_hbm, lab_ref, sol_hbm, res_hbm, f_hi, f_lo, stage, *rest):
        d, part, whole, probs, tan0, b_, zpart, zwhole, zcore, zland, land, outs = (
            rest[2 * n : 2 * n + 2] for n in range(12)
        )
        load_sem, out_sem, send_sem, recv_sem, zsend_sem, zrecv_sem = rest[24:]
        clip, feat = lax.axis_index("clip"), lax.axis_index("feat")
        y, x = clip // RING, clip % RING
        z, core = feat // 2, feat % 2

        def at_x(step):
            return (y * RING + (x + step) % RING, feat)

        def at_y(step):
            return (((y + step) % RING) * RING + x, feat)

        def at_z(step):
            return (clip, ((z + step) % RING) * 2 + core)

        other = (clip, z * 2 + 1 - core)
        x_ring, y_ring = (x, at_x(3), at_x(1)), (y, at_y(3), at_y(1))

        w_pieces = []
        for c in range(2):
            top = up(s.chunks[c] // 2, 16)
            w_pieces += [(c, 0, top), (c, top, s.chunks[c] - top)]

        def load_w(n):
            c, off, size = w_pieces[n]
            return pltpu.make_async_copy(
                w_hbm.at[pl.ds(s.offs[c] + off, size)],
                stage.at[n, pl.ds(0, size)],
                load_sem.at[n],
            )

        def load_f(n, slot):
            return pltpu.make_async_copy(
                f_hbm.at[at(n * STAGE, STAGE)], stage.at[slot], load_sem.at[slot]
            )

        for n in range(SLOTS):
            load_w(n).start()
        peers = [at_x(1), at_x(3), at_y(1), at_y(3), at_z(1), at_z(2), at_z(3), other]
        barrier = pltpu.get_barrier_semaphore()
        for peer in peers:
            pl.semaphore_signal(
                barrier, inc=1, device_id=peer, device_id_type=pl.DeviceIdType.MESH
            )

        for c in range(2):
            pad = 2 * s.side[c] - s.mark[c]
            part[c][pl.ds(s.mark[c], pad)] = jnp.zeros((pad, LANES), jnp.float32)
            pad = s.zall[c] - s.zmark[c]
            for rb in range(ROW_BLOCKS):
                zpart[c][pl.ds(rb * s.zall[c] + s.zmark[c], pad)] = jnp.zeros(
                    (pad, LANES), jnp.float32
                )

        def z_copy(c, rb, n, src, dst, to):
            sem = (c * ROW_BLOCKS + rb) * 8 + n
            return pltpu.make_async_remote_copy(
                src_ref=src,
                dst_ref=dst,
                send_sem=zsend_sem.at[sem],
                recv_sem=zrecv_sem.at[sem],
                device_id=to,
                device_id_type=pl.DeviceIdType.MESH,
            )

        def z_own(c, rb):
            return rb * s.zall[c] + core * s.zhalf[c]

        def z_core(c, rb):
            half = s.zhalf[c]
            src = zpart[c].at[at(rb * s.zall[c] + (1 - core) * half, half)]
            return z_copy(c, rb, 0, src, zcore[c].at[at(rb * half, half)], other)

        def z_land(c, rb, step):
            return zland[c].at[at((rb * 3 + step - 1) * s.zseg[c], s.zseg[c])]

        def z_out(c, rb, step):
            src = zpart[c].at[at(z_own(c, rb) + (z + step) % RING * s.zseg[c], s.zseg[c])]
            return z_copy(c, rb, step, src, z_land(c, rb, step), at_z(step))

        def z_mine(c, rb):
            return at(z_own(c, rb) + z * s.zseg[c], s.zseg[c])

        def z_all(c, rb, step):
            ref = zwhole[c].at[z_mine(c, rb)]
            return z_copy(c, rb, 3 + step, ref, ref, at_z(step))

        def z_back(c, rb):
            ref = zwhole[c].at[at(z_own(c, rb), s.zhalf[c])]
            return z_copy(c, rb, 7, ref, ref, other)

        def forward(c, rb):
            rows = pl.ds(pl.multiple_of(rb * s.rb_rows, s.rb_rows), s.rb_rows)
            value = dot3(d[c][...], s.chunks[c], f_hi[rows], f_lo[rows], NT)
            for b in range(s.rb_blocks):
                zpart[c][at(rb * s.zall[c] + b * s.chunks[c], s.chunks[c])] = value[
                    :, b * LANES : (b + 1) * LANES
                ]
            z_core(c, rb).start()

        def forwards(c):
            lax.fori_loop(0, ROW_BLOCKS, lambda rb, _: (forward(c, rb), 0)[1], 0)

        def z_step1(c):
            for rb in range(ROW_BLOCKS):
                z_core(c, rb).wait_recv()
                rows = at(z_own(c, rb), s.zhalf[c])
                zpart[c][rows] = zpart[c][rows] + zcore[c][at(rb * s.zhalf[c], s.zhalf[c])]
                for step in (2, 1, 3):
                    z_out(c, rb, step).start()

        def z_step2(c):
            for rb in range(ROW_BLOCKS):
                for step in (1, 2, 3):
                    z_out(c, rb, step).wait_recv()
                rows = z_mine(c, rb)
                one, two, three = (z_land(c, rb, step)[...] for step in (1, 2, 3))
                zwhole[c][rows] = (zpart[c][rows] + one) + (two + three)
                for step in (2, 1, 3):
                    z_all(c, rb, step).start()

        def z_step3(c):
            for rb in range(ROW_BLOCKS):
                for step in (1, 2, 3):
                    z_all(c, rb, step).wait_recv()
                z_back(c, rb).start()

        def z_sent(c):
            for rb in range(ROW_BLOCKS):
                z_core(c, rb).wait_send()
                for step in (1, 2, 3):
                    z_out(c, rb, step).wait_send()
                    z_all(c, rb, step).wait_send()
                z_back(c, rb).wait_send()

        def row_carried(n):
            return total(zwhole[1][pl.ds(s.zmark[1] + 8 * n, 8)])

        def lane_block(c, lb):
            return at(lb * s.chunks[c], s.chunks[c])

        def backward_block(c, rows, new):
            stack = b_[c][:, rows]
            for pair in range(0, s.blocks, 2):
                lanes = pl.ds(pair * LANES, 2 * LANES)
                value = dot3(stack, s.chunks[c], f_hi[rows, lanes], f_lo[rows, lanes], NN)
                for b in range(2):
                    to = lane_block(c, pair + b)
                    term = value[:, b * LANES : (b + 1) * LANES]
                    part[c][to] = term if new is True else jnp.where(new, term, part[c][to] + term)

        def finish(work):
            def body(rb, curve):
                for c in range(2):
                    z_back(c, rb).wait_recv()
                for b in range(s.rb_blocks):
                    sums = [
                        zwhole[c][at(rb * s.zall[c] + b * s.chunks[c], s.chunks[c])]
                        for c in range(2)
                    ]
                    lb = rb * s.rb_blocks + b
                    values, tile = work(lb, sums)
                    curve = curve + tile
                    lanes = pl.ds(pl.multiple_of(lb * LANES, LANES), LANES)
                    for c in range(2):
                        high, low = split(values[c])
                        b_[c][pl.ds(0, s.chunks[c]), lanes] = high
                        b_[c][pl.ds(s.chunks[c], s.chunks[c]), lanes] = low
                rows = pl.ds(pl.multiple_of(rb * s.rb_rows, s.rb_rows), s.rb_rows)
                backward_block(0, rows, rb == 0)
                return curve

            return lax.fori_loop(0, ROW_BLOCKS, body, jnp.zeros((8, LANES), jnp.float32))

        class Clip:
            def __init__(self, sems, c, turn, scale):
                self.red1, self.red2, self.gat2, self.gat1 = [], [], [], []
                self.c, self.turn, self.scale = c, turn, scale
                for q, (one, two) in enumerate(((x_ring, y_ring), (y_ring, x_ring))):
                    start, seg, sub = q * s.side[c], s.seg[c], s.sub[c]
                    own = start + one[0] * seg
                    place = q * 3 * (seg + sub)
                    self.red1.append(Reduce(sems, one, part[c], start, seg, land[c], place))
                    self.red2.append(
                        Reduce(sems, two, part[c], own, sub, land[c], place + 3 * seg)
                    )
                    self.gat2.append(Gather(sems, two, whole[c].at[turn], own, sub))
                    self.gat1.append(Gather(sems, one, whole[c].at[turn], start, seg))

            def keep(self, rows, value):
                part[self.c][rows] = value

            def store(self, rows, value):
                whole[self.c].at[self.turn][rows] = value * self.scale

            def r1_first(self):
                for r in self.red1:
                    r.first()

            def r1_near(self):
                for r in self.red1:
                    r.near(True)

            def r1_second(self):
                for r in self.red1:
                    r.second()

            def r1_last(self):
                for r, n in zip(self.red1, self.red2):
                    r.last(self.keep)
                    n.first()
                    n.near(False)

            def r2_second(self):
                for r in self.red2:
                    r.second()

            def r2_last(self):
                for r, n in zip(self.red2, self.gat2):
                    r.last(self.store)
                    n.first()
                    n.near(False)

            def g2_second(self):
                for r in self.gat2:
                    r.second()

            def g2_last(self):
                for r, n in zip(self.gat2, self.gat1):
                    r.last()
                    n.first()

            def g1_near(self):
                for r in self.gat1:
                    r.near(True)

            def g1_second(self):
                for r in self.gat1:
                    r.second()

            def g1_last(self):
                for r in self.gat1:
                    r.last()

            def sent(self):
                for q in range(2):
                    self.red1[q].sent(True)
                    self.red2[q].sent(False)
                    self.gat2[q].sent(False)
                    self.gat1[q].sent(True)

        def sum_over_clip(turn, scale, ready0):
            sems = Sems(send_sem, recv_sem)
            zero, one = Clip(sems, 0, turn, scale), Clip(sems, 1, turn, scale)
            zero.r1_first()
            backward_block(1, pl.ds(0, rows_dev), True)
            zero.r1_near()
            zero.r1_second()
            one.r1_first()
            zero.r1_last()
            one.r1_near()
            one.r1_second()
            zero.r2_second()
            zero.r2_last()
            one.r1_last()
            zero.g2_second()
            one.r2_second()
            zero.g2_last()
            one.r2_last()
            zero.g1_near()
            one.g2_second()
            zero.g1_second()
            one.g2_last()
            zero.g1_last()
            one.g1_near()
            ready0()
            one.g1_second()
            return zero, one

        def sum_over_feat_0():
            z_step1(0)
            z_step2(0)

        def sum_over_feat_1():
            forwards(1)
            z_step3(0)
            z_step1(1)
            z_step2(1)
            z_step3(1)

        def feats(c, turn, block):
            return whole[c][turn, lane_block(c, block)]

        def carried(turn):
            return total(whole[0][turn, pl.ds(s.mark[0], 8)])

        def direct(c, block, value):
            lanes = pl.ds(block * LANES, LANES)
            high, low = split(value)
            d[c][pl.ds(0, s.chunks[c]), lanes] = high
            d[c][pl.ds(s.chunks[c], s.chunks[c]), lanes] = low

        for n in range(SLOTS):
            load_w(n).wait()
            c, off, size = w_pieces[n]
            high, low = split(stage[n, pl.ds(0, size)])
            d[c][pl.ds(off, size)], d[c][pl.ds(s.chunks[c] + off, size)] = high, low
            load_f(n, n).start()
        pl.semaphore_wait(barrier, len(peers))

        def logits_rows(rb, _):
            for n in range(2):
                piece = 2 * rb + n
                slot = piece % SLOTS
                load_f(piece, slot).wait()
                rows = at(piece * STAGE, STAGE)
                f_hi[rows], f_lo[rows] = split(stage[slot])

                @pl.when(rb == 0)
                def _():
                    load_f(SLOTS + n, n).start()

            forward(0, rb)
            forward(1, rb)
            return 0

        lax.fori_loop(0, ROW_BLOCKS, logits_rows, 0)
        for c in range(2):
            z_step1(c)
        for c in range(2):
            z_step2(c)
        for c in range(2):
            z_step3(c)

        def softmax_rows(lb, sums):
            top = jnp.maximum(
                jnp.max(sums[0], axis=0, keepdims=True), jnp.max(sums[1], axis=0, keepdims=True)
            )
            grown = [jnp.exp(v - top) for v in sums]
            scale = jnp.sum(grown[0], axis=0, keepdims=True) + jnp.sum(
                grown[1], axis=0, keepdims=True
            )
            hit = lab_ref[pl.ds(lb, 1), :]
            values = []
            for c in range(2):
                prob = grown[c] / scale
                probs[c][lane_block(c, lb)] = prob
                which = lax.broadcasted_iota(jnp.int32, (s.chunks[c], LANES), 0) + s.offs[c]
                values.append(prob - jnp.where(which == hit, 1.0, 0.0))
            return values, jnp.zeros((8, LANES), jnp.float32)

        finish(softmax_rows)
        for c in range(2):
            z_sent(c)

        def negated(c):
            norm = jnp.zeros((8, LANES), jnp.float32)
            for block in range(s.blocks):
                value = feats(c, 0, block)
                norm = norm + tile_sum(value * value)
                direct(c, block, value)
            return norm

        norms = []

        def ready0():
            norms.append(negated(0))
            forwards(0)

        zero, one = sum_over_clip(0, -1.0 / total_rows, ready0)
        sum_over_feat_0()
        one.g1_last()
        zpart[1][pl.ds(s.zmark[1], 8)] = norms[0] + negated(1)
        sum_over_feat_1()
        zero.sent()
        one.sent()

        def bend(lb, tangents):
            prob = [probs[c][lane_block(c, lb)] for c in range(2)]
            weighted = [p * t for p, t in zip(prob, tangents)]
            mean = jnp.sum(weighted[0], axis=0, keepdims=True) + jnp.sum(
                weighted[1], axis=0, keepdims=True
            )
            bent = [w - p * mean for w, p in zip(weighted, prob)]
            return bent, tile_sum(bent[0] * tangents[0]) + tile_sum(bent[1] * tangents[1])

        def first_rows(lb, sums):
            for c in range(2):
                tan0[c][lane_block(c, lb)] = sums[c]
            return bend(lb, sums)

        part[0][pl.ds(s.mark[0], 8)] = finish(first_rows)
        for c in range(2):
            z_sent(c)
        norm0 = row_carried(0)

        def residual1(c, block, step0):
            first = feats(c, 0, block)
            return first, first - step0 * (feats(c, 1, block) + damping * first)

        def first_step():
            return norm0 / (carried(1) + damping * norm0)

        def stepped(c):
            step0 = first_step()
            norm = jnp.zeros((8, LANES), jnp.float32)
            cross = jnp.zeros((8, LANES), jnp.float32)
            for block in range(s.blocks):
                first, value = residual1(c, block, step0)
                norm = norm + tile_sum(value * value)
                cross = cross + tile_sum(value * first)
                direct(c, block, value)
            return norm, cross

        def ready1():
            norms[:] = stepped(0)
            forwards(0)

        zero, one = sum_over_clip(1, 1.0 / total_rows, ready1)
        sum_over_feat_0()
        one.g1_last()
        norm, cross = stepped(1)
        zpart[1][pl.ds(s.zmark[1], 8)] = norms[0] + norm
        zpart[1][pl.ds(s.zmark[1] + 8, 8)] = norms[1] + cross
        sum_over_feat_1()
        zero.sent()
        one.sent()

        def second_rows(lb, sums):
            beta = row_carried(0) / norm0
            return bend(
                lb, [sums[c] + beta * tan0[c][lane_block(c, lb)] for c in range(2)]
            )

        part[0][pl.ds(s.mark[0], 8)] = finish(second_rows)
        for c in range(2):
            z_sent(c)

        def out_copies(c):
            return [
                pltpu.make_async_copy(
                    outs[n].at[pl.ds(s.offs[c], s.chunks[c])],
                    (sol_hbm, res_hbm)[n].at[pl.ds(s.offs[c], s.chunks[c])],
                    out_sem.at[2 * c + n],
                )
                for n in range(2)
            ]

        def results(c):
            norm1 = row_carried(0)
            beta = norm1 / norm0
            length = norm1 + 2.0 * beta * row_carried(1) + beta * beta * norm0
            step0 = first_step()
            step1 = norm1 / (carried(2) + damping * length)
            rows = pl.ds(s.offs[c], s.chunks[c])
            for block in range(s.blocks):
                first, value = residual1(c, block, step0)
                direction = value + beta * first
                lanes = pl.ds(block * LANES, LANES)
                outs[0][rows, lanes] = step0 * first + step1 * direction
                outs[1][rows, lanes] = step1 * (feats(c, 2, block) + damping * direction) - value
            for copy in out_copies(c):
                copy.start()

        zero, one = sum_over_clip(2, 1.0 / total_rows, lambda: results(0))
        one.g1_last()
        results(1)
        zero.sent()
        one.sent()
        for c in range(2):
            for copy in out_copies(c):
                copy.wait()

    return kernel


def local(features, weights, labels):
    rows_dev, feats_dev = features.shape
    classes = weights.shape[0]
    total_rows = rows_dev * lax.axis_size("clip")
    s = Sizes(rows_dev, feats_dev, classes)
    f32, bf16 = jnp.float32, jnp.bfloat16

    def rows(n):
        return pltpu.VMEM((n, LANES), f32)

    def each(make):
        return [make(0), make(1)]

    scratch = [
        pltpu.VMEM((rows_dev, feats_dev), bf16),
        pltpu.VMEM((rows_dev, feats_dev), bf16),
        pltpu.VMEM((SLOTS, STAGE, feats_dev), f32),
        *each(lambda c: pltpu.VMEM((2 * s.chunks[c], feats_dev), bf16)),
        *each(lambda c: rows(2 * s.side[c])),
        *each(lambda c: pltpu.VMEM((TURNS, 2 * s.side[c], LANES), f32)),
        *each(lambda c: rows(s.row_lanes * s.chunks[c])),
        *each(lambda c: rows(s.row_lanes * s.chunks[c])),
        *each(lambda c: pltpu.VMEM((2 * s.chunks[c], rows_dev), bf16)),
        *each(lambda c: rows(ROW_BLOCKS * s.zall[c])),
        *each(lambda c: rows(ROW_BLOCKS * s.zall[c])),
        *each(lambda c: rows(ROW_BLOCKS * s.zhalf[c])),
        *each(lambda c: rows(ROW_BLOCKS * 3 * s.zseg[c])),
        *each(lambda c: rows(2 * 3 * (s.seg[c] + s.sub[c]))),
        *each(lambda c: pltpu.VMEM((classes, feats_dev), f32)),
        pltpu.SemaphoreType.DMA((SLOTS,)),
        pltpu.SemaphoreType.DMA((4,)),
        pltpu.SemaphoreType.DMA((96,)),
        pltpu.SemaphoreType.DMA((96,)),
        pltpu.SemaphoreType.DMA((48,)),
        pltpu.SemaphoreType.DMA((48,)),
    ]
    moved, against = pl.pallas_call(
        make_kernel(s, rows_dev, classes, total_rows),
        name="steps",
        out_shape=[jax.ShapeDtypeStruct(weights.shape, f32)] * 2,
        in_specs=[
            pl.BlockSpec(memory_space=pl.ANY),
            pl.BlockSpec(memory_space=pl.ANY),
            pl.BlockSpec(memory_space=pltpu.VMEM),
        ],
        out_specs=[pl.BlockSpec(memory_space=pl.ANY)] * 2,
        scratch_shapes=scratch,
        compiler_params=pltpu.CompilerParams(
            collective_id=0, has_side_effects=True, vmem_limit_bytes=67_000_000
        ),
    )(features, weights, labels.reshape(s.row_lanes, LANES))
    return weights + moved, -against


def solution(mesh):
    in_specs = (P("clip", "feat"), P(None, "feat"), P("clip"))
    out_specs = (P(None, "feat"), P(None, "feat"))
    return jax.shard_map(local, mesh=mesh, in_specs=in_specs, out_specs=out_specs, check_vma=False)
```

time: 645 us -> 261 us (0.40); the launches traced: 637 us -> 261 us
  waiting for transfers between devices: 334 us -> 0 us
  Pallas kernels: 0 us -> 251 us
  blocking collectives: 153 us -> 0 us
  matrix products: 97.9 us -> 0 us
  between operations: 19.6 us -> 0.65 us
  other arithmetic: 23.6 us -> 8.82 us
    psum x3 -> x0, waiting for transfers between devices: 313 us -> none  [backward(): return lax.psum(contract_rows(row_values, features) / total_rows, 'clip')]
    pallas_call x0 -> x1, Pallas kernels: none -> 251 us  [local(): pl.pallas_call(make_kernel(s, rows_dev, classes, total_rows), name='steps...]
    all_to_all x5 -> x0, blocking collectives: 122 us -> none  [the longest x3 72.3 us: from_everyone(): lax.all_to_all(jnp.broadcast_to(array[None], (count, *array.shape)), axis...]
    dot_general x5 -> x0, matrix products: 79.4 us -> none  [the longest x3 48 us: contract_rows(): lax.dot_general(left, right, (((0,), (0,)), ((), ())), precision=lax.Prec...]
    psum x2 -> x0, blocking collectives: 30.5 us -> none  [local(): lax.psum((jnp.sum(residual * residual), jnp.sum(direction * image), jnp.s...]
    all_to_all x1 -> x0, waiting for transfers between devices: 20.7 us -> none  [sent_and_summed(): lax.all_to_all(blocks, axis, split_axis=0, concat_axis=0, tiled=True)]
    reshape x1 -> x0, matrix products: 18.5 us -> none  [cut_along(): array.reshape(*dims[:dim], count, dims[dim] // count, *dims[dim + 1:])]
    reduce_sum x8 -> x0, other arithmetic: 12.7 us -> none  [the longest x1 6.48 us: local(): jnp.sum(direction * image)]
  transfers between devices with their start and end apart: 4 -> 0, of which waited for: 4 -> 0; matrix products, arithmetic and copies ran while one was open for 0% -> 0% of each run, Pallas kernels for 0% -> 0%
where the time goes in v1:
time: 261 us
  Pallas kernels  251 us (96%)
  other arithmetic  8.82 us (3%)
    pallas_call x1, Pallas kernels, local(): pl.pallas_call(make_kernel(s, rows_dev, classes, total_rows), name='steps...  251 us
    add x1, other arithmetic, local(): return (weights + moved, -against)  6.41 us

profile of v1, /device:TPU:0, one launch (start us, length us, event | category | flops | bytes accessed | tf_op | source)
XLA Modules:
  0.0 260.9 jit_solution(5255161733090778785)
XLA Ops:
  0.6 251.4 %steps.1 = (f32[400,2816]{1,0:T(8,128)}, f32[400,2816]{1,0:T(8,128)}) custom-call(f32[768,2816]{1,0:T(8,128)} %f_hbm.1, f32[400,2816]{1,0:T(8,128)} %w_hbm.1, s32[6,128]{1,0:T(8,128)} %bitcast.1), custom_call_target="tpu_custom_call" | custom-call | tf_op jit(solution)/shard_map/steps/pallas_call | solution.py:717
  252.0 0.0 copy-start
  252.1 6.4 %add.3 = f32[400,2816]{1,0:T(8,128)} add(f32[400,2816]{1,0:T(8,128)} %w_hbm.1, f32[400,2816]{1,0:T(8,128)} %get-tuple-element.4) | non-fusion elementwise | flops 1126400 | bytes 13516800 | tf_op jit(solution)/shard_map/add | solution.py:732
  258.5 0.0 copy-done
  258.5 2.4 neg.3
Async XLA Ops:
  252.0 6.4 %copy-start = (f32[400,2816]{1,0:T(8,128)S(1)}, f32[400,2816]{1,0:T(8,128)}, u32[]{:S(2)}) copy-start(f32[400,2816]{1,0:T(8,128)} %get-tuple-element.5) | copy-start | bytes 13516804
